TPU v7x, 256 devices: a whole 4x4x8 slice. The times are simulated.
256 devices in a mesh: gy: 32 (over z, y), gx: 8 (over x, core).
Axes of the slice: x: 4, y: 4, z: 8, core: 2. Of those that a mesh axis runs over, the one named last changes fastest.
Arguments:
- bins: int32 [4, 512, 8192], P(None, 'gy', 'gx'), may hold values from 0 to 4095
- mask: int32 [4, 512, 8192], P(None, 'gy', 'gx'), may hold values from 0 to 1
- atlas: bfloat16 [8, 4, 512, 8192], P(None, None, 'gy', 'gx'), may hold values from -100 to 130
- init_mean: float32 [8], replicated, may hold values from 0.05 to 0.95
- init_scale: float32 [8], replicated, may hold values from 0.004 to 0.15
Outputs:
- phase_prob: bfloat16 [8, 4, 512, 8192], P(None, None, 'gy', 'gx')
- em_params: float32 [3, 8], replicated
- bin_density: float32 [4096], P(('gy', 'gx'))
All inputs are finite; a program needn't handle non-finite values.
Results may differ from a plain program's by a relative error of at most 0.0015.
Values may be sent and summed in bfloat16 or wider, within the bound.
A program may use at most 64 MiB of HBM per device.

v0:
```python
import math
import jax
import jax.numpy as jnp
from jax import lax
from jax.sharding import PartitionSpec as P

NB = 4096
EM_ITERS = 5
POTTS = 3
VAR_EPS = 1e-05
BETA = 0.3


def extended(x, sides, width):
    for axis, dim in sides:
        size, length = (lax.axis_size(axis), x.shape[dim])
        up = [(i, (i + 1) % size) for i in range(size - 1)]
        down = [(j, i) for i, j in up]
        last = lax.slice_in_dim(x, length - width, length, axis=dim)
        initial = lax.slice_in_dim(x, 0, width, axis=dim)
        before = lax.ppermute(last, axis, up)
        after = lax.ppermute(initial, axis, down)
        x = jnp.concatenate([before, x, after], axis=dim)
    return x


def phase_scores(values, mean, var, weight):
    shape = (mean.shape[0],) + (1,) * values.ndim
    m = mean.reshape(shape)
    v = var.reshape(shape)
    w = weight.reshape(shape)
    diff = values[None] - m
    return jnp.log(w) - 0.5 * jnp.log(v) - diff * diff / (2.0 * v)


def moments(counts, centers, mean, var, weight):
    resp = jax.nn.softmax(phase_scores(centers, mean, var, weight), axis=0)
    weighted = resp * counts[None]
    return jnp.stack(
        [
            jnp.sum(weighted, 1),
            jnp.sum(weighted * centers[None], 1),
            jnp.sum(weighted * (centers * centers)[None], 1),
        ]
    )


def refit(sums, count_phases):
    occ, first, second = (sums[0], sums[1], sums[2])
    mean = first / (occ + 1.0)
    var = (second - first * mean) / (occ + 1.0) + VAR_EPS
    weight = (occ + 1.0) / (jnp.sum(occ) + count_phases)
    return (mean, var, weight)


def cycle_total(padded, rows, cols):
    total = jnp.zeros(padded.shape[:2] + (rows, cols), jnp.float32)
    for dy in range(-2, 3):
        for dx in range(-2, 3):
            if dy != 0 or dx != 0:
                piece = padded[:, :, 2 + dy : 2 + dy + rows, 2 + dx : 2 + dx + cols].astype(
                    jnp.float32
                )
                total = total + piece * (1.0 / (dy * dy + dx * dx))
    return total


def plane_total(held):
    padded = jnp.pad(held.astype(jnp.float32), ((0, 0), (1, 1), (0, 0), (0, 0)))
    return padded[:, :-2] + padded[:, 2:]


def per_device(bins, mask, atlas, init_mean, init_scale):
    planes, rows, cols = bins.shape
    phases = init_mean.shape[0]
    devices_all = lax.axis_size("gy") * lax.axis_size("gx")
    scale_factor = float(NB) / float(planes * rows * cols * devices_all)
    group = math.gcd(16, planes * rows)
    block_bins = bins.reshape(-1, group * cols)
    block_mask = mask.reshape(-1, group * cols)
    high_count = NB // 128

    def count_block(acc, item):
        part_bins, part_mask = item
        high = part_bins // 128
        low = part_bins % 128
        high_hot = (high[None, :] == jnp.arange(high_count, dtype=jnp.int32)[:, None]).astype(
            jnp.bfloat16
        )
        high_hot = high_hot * part_mask.astype(jnp.bfloat16)[None, :]
        low_hot = (low[None, :] == jnp.arange(128, dtype=jnp.int32)[:, None]).astype(jnp.bfloat16)
        table = lax.dot_general(
            high_hot, low_hot, (((1,), (1,)), ((), ())), preferred_element_type=jnp.float32
        )
        return (acc + table, None)

    table, _ = lax.scan(
        count_block, jnp.zeros((high_count, 128), jnp.float32), (block_bins, block_mask)
    )
    counts = table.reshape(NB)
    mean = init_mean
    var = init_scale * init_scale
    weight = jnp.full((phases,), 1.0 / phases, jnp.float32)
    share = lax.psum_scatter(counts, ("gy", "gx"), scatter_dimension=0, tiled=True)
    start = lax.axis_index(("gy", "gx")) * share.shape[0]
    density = share * scale_factor
    centers = ((start + jnp.arange(share.shape[0], dtype=jnp.int32)).astype(jnp.float32) + 0.5) / NB
    for step in range(EM_ITERS):
        sums = lax.psum(moments(share, centers, mean, var, weight), ("gy", "gx"))
        mean, var, weight = refit(sums, float(phases))
    params = jnp.stack([mean, var, weight])
    intensity = (bins.astype(jnp.float32) + 0.5) / NB
    unary = phase_scores(intensity, mean, var, weight) + atlas.astype(jnp.float32)
    fg = mask.astype(jnp.float32)
    q = jax.nn.softmax(unary, axis=0).astype(jnp.bfloat16)
    for step in range(POTTS):
        held = (q.astype(jnp.float32) * fg[None]).astype(jnp.bfloat16)
        padded = extended(held, (("gy", 2), ("gx", 3)), 2)
        field = cycle_total(padded, rows, cols) + plane_total(held)
        q = jax.nn.softmax(unary + BETA * field, axis=0).astype(jnp.bfloat16)
    phase_prob = (q.astype(jnp.float32) * fg[None]).astype(jnp.bfloat16)
    return (phase_prob, params, density)


def solution(mesh):
    in_specs = (P(None, "gy", "gx"), P(None, "gy", "gx"), P(None, None, "gy", "gx"), P(), P())
    out_specs = (P(None, None, "gy", "gx"), P(), P(("gy", "gx")))
    return jax.shard_map(
        per_device, mesh=mesh, in_specs=in_specs, out_specs=out_specs, check_vma=False
    )
```

profile of v0, /device:TPU:121, one launch (start us, length us, event | category | flops | bytes accessed | tf_op | source)
XLA Modules:
  0.0 586.1 jit_solution(10782457312624884916)
XLA Ops:
  0.7 0.7 multiply_subtract_fusion
  1.3 0.7 fusion.37
  2.1 0.7 fusion.28
  2.8 1.1 copy.9
  4.0 1.1 copy.8
  5.1 10.4 %while.13 = (s32[]{:T(128)}, f32[32,128]{1,0:T(8,128)S(1)}, s32[4,16384]{1,0:T(4,128)S(1)}, s32[4,16384]{1,0:T(4,128)S(1)}, s32[]{:T(128)}, /*index=5*/s32[]{:T(128)}) while((s32[]{:T(128)}, f32[32,128]{1,0:T(8,128)S(1)}, s32[4,16384]{1,0:T(4,128)S(1)}, s32[4,16384]{1,0:T(4,128)S(1)}, s32[]{:T(128)}, /*index=5*/s32[]{:T(128)}) %tuple.78), condition=%wide.region_3.4_spmd.clone, body=%wide.region_2.3_spmd.clone.sunk | while | flops 137715712 | bytes 2719839 | solution.py:97
  6.0 1.7 fusion.95
  8.6 1.7 fusion.95
  11.2 1.7 fusion.95
  13.8 1.7 fusion.95
  15.5 75.7 %all-reduce.3 = f32[4096]{0:T(1024)S(1)} all-reduce(f32[4096]{0:T(1024)S(1)} %bitcast.175), channel_id=2, replica_groups=mesh['gy'=32,'gx'=8] {'gy','gx'}, use_global_device_ids=true, to_apply=%region_4.5.clone | all-reduce | flops 4096 | bytes 32768
  92.1 73.5 %psum.35 = f32[3,8]{1,0:T(4,128)S(1)} all-reduce(f32[3,8]{1,0:T(4,128)S(1)} %pad_maximum_fusion.18), channel_id=1, replica_groups=mesh['gy'=32,'gx'=8] {'gy','gx'}, use_global_device_ids=true, to_apply=%region_8.9 | all-reduce | flops 24 | bytes 192 | tf_op jit(solution)/shard_map/psum | solution.py:109
  165.5 0.6 slice_reduce_fusion.4
  167.3 74.1 %psum.36 = f32[3,8]{1,0:T(4,128)S(1)} all-reduce(f32[3,8]{1,0:T(4,128)S(1)} %pad_maximum_fusion.19), channel_id=1, replica_groups=mesh['gy'=32,'gx'=8] {'gy','gx'}, use_global_device_ids=true, to_apply=%region_15.16 | all-reduce | flops 24 | bytes 192 | tf_op jit(solution)/shard_map/psum | solution.py:109
  241.4 0.6 slice_reduce_fusion.3
  243.1 73.5 %psum.37 = f32[3,8]{1,0:T(4,128)S(1)} all-reduce(f32[3,8]{1,0:T(4,128)S(1)} %pad_maximum_fusion.20), channel_id=1, replica_groups=mesh['gy'=32,'gx'=8] {'gy','gx'}, use_global_device_ids=true, to_apply=%region_22.23 | all-reduce | flops 24 | bytes 192 | tf_op jit(solution)/shard_map/psum | solution.py:109
  316.5 0.6 slice_reduce_fusion.2
  318.3 74.1 %psum.38 = f32[3,8]{1,0:T(4,128)S(1)} all-reduce(f32[3,8]{1,0:T(4,128)S(1)} %pad_maximum_fusion.21), channel_id=1, replica_groups=mesh['gy'=32,'gx'=8] {'gy','gx'}, use_global_device_ids=true, to_apply=%region_29.30 | all-reduce | flops 24 | bytes 192 | tf_op jit(solution)/shard_map/psum | solution.py:109
  392.4 0.6 slice_reduce_fusion.1
  394.2 73.5 %psum.39 = f32[3,8]{1,0:T(4,128)S(1)} all-reduce(f32[3,8]{1,0:T(4,128)S(1)} %pad_maximum_fusion.22), channel_id=1, replica_groups=mesh['gy'=32,'gx'=8] {'gy','gx'}, use_global_device_ids=true, to_apply=%region_36.37 | all-reduce | flops 24 | bytes 192 | tf_op jit(solution)/shard_map/psum | solution.py:109
  467.6 0.6 fusion.63
  469.5 0.7 fusion.18
  470.2 0.9 multiply_convert_fusion.3
  471.4 4.0 collective-permute-start
  475.4 1.9 collective-permute-start.1
  477.6 6.8 %collective-permute-done.1 = bf16[8,4,2,1024]{3,2,1,0:T(2,128)(2,1)S(1)} collective-permute-done((bf16[8,4,2,1024]{3,2,1,0:T(2,128)(2,1)S(1)}, bf16[8,4,2,1024]{3,2,1,0:T(2,128)(2,1)S(1)}, u32[]{:S(2)}, u32[]{:S(2)}) %collective-permute-start.1) | collective-permute-done | bytes 131104 | tf_op jit(solution)/shard_map/ppermute | solution.py:22
  484.7 4.7 collective-permute-start.2
  489.4 2.1 collective-permute-start.3
  492.0 4.4 collective-permute-done.3
  496.4 2.9 maximum_maximum_fusion
  499.2 11.3 %fusion.75 = (f32[4,16,1024]{2,1,0:T(8,128)S(1)}, f32[8,4,16,1024]{3,2,1,0:T(8,128)S(1)}) fusion(f32[8,6,16,1024]{3,2,1,0:T(8,128)S(1)} %pad_convert_fusion.2, bf16[8,4,20,1026]{3,2,1,0:T(8,128)(2,1)S(1)} %get-tuple-element.134, bf16[8,4,2,1024]{3,2,1,0:T(2,128)(2,1)S(1)} %collective-permute-done.1, bf16[8,4,16,1024]{3,2,1,0:T(8,128)(2,1)S(1)} %multiply_convert_fusion.3, ...), kind=kLoop, calls=%fused_computation.201 | loop fusion | flops 47120384 | bytes 30146656 | tf_op jit(solution)/shard_map/reduce_max | solution.py:120
  511.5 1.9 collective-permute-start.4
  513.4 3.4 collective-permute-start.5
  517.2 5.2 collective-permute-done.5
  522.7 4.0 collective-permute-start.6
  526.7 1.9 collective-permute-start.7
  529.3 4.4 collective-permute-done.7
  533.7 2.9 maximum_maximum_fusion.1
  536.5 11.3 %fusion.73 = (f32[4,16,1024]{2,1,0:T(8,128)S(1)}, f32[8,4,16,1024]{3,2,1,0:T(8,128)S(1)}) fusion(f32[8,6,16,1024]{3,2,1,0:T(8,128)S(1)} %pad_convert_fusion.1, bf16[8,4,20,1026]{3,2,1,0:T(8,128)(2,1)S(1)} %get-tuple-element.130, bf16[8,4,2,1024]{3,2,1,0:T(2,128)(2,1)S(1)} %collective-permute-done.5, bf16[8,4,16,1024]{3,2,1,0:T(8,128)(2,1)S(1)} %multiply_convert_fusion.2, ...), kind=kLoop, calls=%fused_computation.200 | loop fusion | flops 47120384 | bytes 30146656 | tf_op jit(solution)/shard_map/reduce_max | solution.py:120
  548.8 1.9 collective-permute-start.8
  550.7 3.4 collective-permute-start.9
  554.7 5.1 collective-permute-done.9
  560.0 3.3 collective-permute-start.10
  563.3 2.1 collective-permute-start.11
  565.9 4.4 collective-permute-done.11
  570.3 2.9 maximum_maximum_fusion.2
  573.2 11.3 %fusion.71 = (f32[4,16,1024]{2,1,0:T(8,128)S(1)}, f32[8,4,16,1024]{3,2,1,0:T(8,128)S(1)}) fusion(f32[8,6,16,1024]{3,2,1,0:T(8,128)S(1)} %pad_convert_fusion, bf16[8,4,20,1026]{3,2,1,0:T(8,128)(2,1)S(1)} %get-tuple-element.126, bf16[8,4,2,1024]{3,2,1,0:T(2,128)(2,1)S(1)} %collective-permute-done.9, bf16[8,4,16,1024]{3,2,1,0:T(8,128)(2,1)S(1)} %multiply_convert_fusion.1, ...), kind=kLoop, calls=%fused_computation.199 | loop fusion | flops 47120384 | bytes 30146656 | tf_op jit(solution)/shard_map/reduce_max | solution.py:120
  584.7 1.4 multiply_convert_fusion
  (80 shorter events, 12.6 us)
Async XLA Ops:
  5.1 86.7 %copy-start.3 = (f32[8]{0:T(128)S(1)}, f32[8]{0:T(128)}, u32[]{:S(2)}) copy-start(f32[8]{0:T(128)} %param.10) | copy-start | bytes 100
  5.1 313.2 %copy-start.1 = (s32[4,16,1024]{2,1,0:T(8,128)S(1)}, s32[4,16,1024]{2,1,0:T(8,128)}, u32[]{:S(2)}) copy-start(s32[4,16,1024]{2,1,0:T(8,128)} %param.7) | copy-start | bytes 786436
  5.1 389.0 %copy-start.2 = (s32[4,16,1024]{2,1,0:T(8,128)S(1)}, s32[4,16,1024]{2,1,0:T(8,128)}, u32[]{:S(2)}) copy-start(s32[4,16,1024]{2,1,0:T(8,128)} %param.8) | copy-start | bytes 786436
  5.1 463.8 %copy-start = (bf16[8,4,16,1024]{3,2,1,0:T(8,128)(2,1)S(1)}, bf16[8,4,16,1024]{3,2,1,0:T(8,128)(2,1)}, u32[]{:S(2)}) copy-start(bf16[8,4,16,1024]{3,2,1,0:T(8,128)(2,1)} %param.9) | copy-start | bytes 3145732
  471.4 6.3 %collective-permute-start = (bf16[8,4,2,1024]{3,2,1,0:T(2,128)(2,1)S(1)}, bf16[8,4,2,1024]{3,2,1,0:T(2,128)(2,1)S(1)}, u32[]{:S(2)}, u32[]{:S(2)}) collective-permute-start(bf16[8,4,2,1024]{3,2,1,0:T(2,128)(2,1)S(1)} %get-tuple-element.141), channel_id=1, source_target_pairs={{0,8},{8,16},{16,24},{24,32},{32,40},{40,48},{48,56},{56,64},{64,7... | collective-permute-start | bytes 393224 | tf_op jit(solution)/shard_map/ppermute | solution.py:21
  475.4 9.0 %collective-permute-start.1 = (bf16[8,4,2,1024]{3,2,1,0:T(2,128)(2,1)S(1)}, bf16[8,4,2,1024]{3,2,1,0:T(2,128)(2,1)S(1)}, u32[]{:S(2)}, u32[]{:S(2)}) collective-permute-start(bf16[8,4,2,1024]{3,2,1,0:T(2,128)(2,1)S(1)} %get-tuple-element.142), channel_id=1, source_target_pairs={{8,0},{16,8},{24,16},{32,24},{40,32},{48,40},{56,48},{64,56},{72,6... | collective-permute-start | bytes 393224 | tf_op jit(solution)/shard_map/ppermute | solution.py:22
  484.7 7.3 %collective-permute-start.2 = (bf16[8,4,20,2]{3,2,1,0:T(8,128)(2,1)S(1)}, bf16[8,4,20,2]{3,2,1,0:T(8,128)(2,1)S(1)}, u32[]{:S(2)}, u32[]{:S(2)}) collective-permute-start(bf16[8,4,20,2]{3,2,1,0:T(8,128)(2,1)S(1)} %get-tuple-element.135), channel_id=1, source_target_pairs={{0,1},{1,2},{2,3},{3,4},{4,5},{5,6},{6,7},{8,9},{9,10},{10,11},{11... | collective-permute-start | bytes 7688 | tf_op jit(solution)/shard_map/ppermute | solution.py:21
  489.4 7.0 %collective-permute-start.3 = (bf16[8,4,20,2]{3,2,1,0:T(8,128)(2,1)S(1)}, bf16[8,4,20,2]{3,2,1,0:T(8,128)(2,1)S(1)}, u32[]{:S(2)}, u32[]{:S(2)}) collective-permute-start(bf16[8,4,20,2]{3,2,1,0:T(8,128)(2,1)S(1)} %get-tuple-element.136), channel_id=1, source_target_pairs={{1,0},{2,1},{3,2},{4,3},{5,4},{6,5},{7,6},{9,8},{10,9},{11,10},{12... | collective-permute-start | bytes 7688 | tf_op jit(solution)/shard_map/ppermute | solution.py:22
  511.5 5.7 collective-permute-start.4
  513.4 9.0 %collective-permute-start.5 = (bf16[8,4,2,1024]{3,2,1,0:T(2,128)(2,1)S(1)}, bf16[8,4,2,1024]{3,2,1,0:T(2,128)(2,1)S(1)}, u32[]{:S(2)}, u32[]{:S(2)}) collective-permute-start(bf16[8,4,2,1024]{3,2,1,0:T(2,128)(2,1)S(1)} %get-tuple-element.140), channel_id=1, source_target_pairs={{8,0},{16,8},{24,16},{32,24},{40,32},{48,40},{56,48},{64,56},{72,6... | collective-permute-start | bytes 393224 | tf_op jit(solution)/shard_map/ppermute | solution.py:22
  522.7 6.6 %collective-permute-start.6 = (bf16[8,4,20,2]{3,2,1,0:T(8,128)(2,1)S(1)}, bf16[8,4,20,2]{3,2,1,0:T(8,128)(2,1)S(1)}, u32[]{:S(2)}, u32[]{:S(2)}) collective-permute-start(bf16[8,4,20,2]{3,2,1,0:T(8,128)(2,1)S(1)} %get-tuple-element.131), channel_id=1, source_target_pairs={{0,1},{1,2},{2,3},{3,4},{4,5},{5,6},{6,7},{8,9},{9,10},{10,11},{11... | collective-permute-start | bytes 7688 | tf_op jit(solution)/shard_map/ppermute | solution.py:21
  526.7 7.0 %collective-permute-start.7 = (bf16[8,4,20,2]{3,2,1,0:T(8,128)(2,1)S(1)}, bf16[8,4,20,2]{3,2,1,0:T(8,128)(2,1)S(1)}, u32[]{:S(2)}, u32[]{:S(2)}) collective-permute-start(bf16[8,4,20,2]{3,2,1,0:T(8,128)(2,1)S(1)} %get-tuple-element.132), channel_id=1, source_target_pairs={{1,0},{2,1},{3,2},{4,3},{5,4},{6,5},{7,6},{9,8},{10,9},{11,10},{12... | collective-permute-start | bytes 7688 | tf_op jit(solution)/shard_map/ppermute | solution.py:22
  548.8 5.9 %collective-permute-start.8 = (bf16[8,4,2,1024]{3,2,1,0:T(2,128)(2,1)S(1)}, bf16[8,4,2,1024]{3,2,1,0:T(2,128)(2,1)S(1)}, u32[]{:S(2)}, u32[]{:S(2)}) collective-permute-start(bf16[8,4,2,1024]{3,2,1,0:T(2,128)(2,1)S(1)} %get-tuple-element.137), channel_id=1, source_target_pairs={{0,8},{8,16},{16,24},{24,32},{32,40},{40,48},{48,56},{56,64},{64,7... | collective-permute-start | bytes 393224 | tf_op jit(solution)/shard_map/ppermute | solution.py:21
  550.7 9.0 %collective-permute-start.9 = (bf16[8,4,2,1024]{3,2,1,0:T(2,128)(2,1)S(1)}, bf16[8,4,2,1024]{3,2,1,0:T(2,128)(2,1)S(1)}, u32[]{:S(2)}, u32[]{:S(2)}) collective-permute-start(bf16[8,4,2,1024]{3,2,1,0:T(2,128)(2,1)S(1)} %get-tuple-element.138), channel_id=1, source_target_pairs={{8,0},{16,8},{24,16},{32,24},{40,32},{48,40},{56,48},{64,56},{72,6... | collective-permute-start | bytes 393224 | tf_op jit(solution)/shard_map/ppermute | solution.py:22
  560.0 5.9 %collective-permute-start.10 = (bf16[8,4,20,2]{3,2,1,0:T(8,128)(2,1)S(1)}, bf16[8,4,20,2]{3,2,1,0:T(8,128)(2,1)S(1)}, u32[]{:S(2)}, u32[]{:S(2)}) collective-permute-start(bf16[8,4,20,2]{3,2,1,0:T(8,128)(2,1)S(1)} %get-tuple-element.127), channel_id=1, source_target_pairs={{0,1},{1,2},{2,3},{3,4},{4,5},{5,6},{6,7},{8,9},{9,10},{10,11},{11... | collective-permute-start | bytes 7688 | tf_op jit(solution)/shard_map/ppermute | solution.py:21
  563.3 7.0 %collective-permute-start.11 = (bf16[8,4,20,2]{3,2,1,0:T(8,128)(2,1)S(1)}, bf16[8,4,20,2]{3,2,1,0:T(8,128)(2,1)S(1)}, u32[]{:S(2)}, u32[]{:S(2)}) collective-permute-start(bf16[8,4,20,2]{3,2,1,0:T(8,128)(2,1)S(1)} %get-tuple-element.128), channel_id=1, source_target_pairs={{1,0},{2,1},{3,2},{4,3},{5,4},{6,5},{7,6},{9,8},{10,9},{11,10},{12... | collective-permute-start | bytes 7688 | tf_op jit(solution)/shard_map/ppermute | solution.py:22
where the time goes:
time: 588 us; the launch traced here: 586 us
  blocking collectives  444 us (76%)
  other arithmetic  61.4 us (10%)
  starting transfers between devices  34.6 us (6%)
  waiting for transfers between devices  31.4 us (5%)
  matrix products  6.88 us (1%)
    psum x5, blocking collectives, per_device(): sums = lax.psum(moments(share, centers, mean, var, weight), ('gy', 'gx'))  369 us
    unnamed x1, blocking collectives  75.7 us
    reduce_max x3, other arithmetic, per_device(): q = jax.nn.softmax(unary + BETA * field, axis=0).astype(jnp.bfloat16)  33.8 us
    ppermute x6, waiting for transfers between devices, extended(): after = lax.ppermute(initial, axis, down)  30.3 us
    ppermute x6, starting transfers between devices, extended(): before = lax.ppermute(last, axis, up)  19.8 us
    ppermute x6, starting transfers between devices, extended(): after = lax.ppermute(initial, axis, down)  14.8 us
  transfers between devices with their start and end apart: 12, of which 11 were waited for; matrix products, arithmetic and copies ran while one was open for 0% of the time, Pallas kernels for 0%

commit v1 on v0

--- a/solution.py
+++ b/solution.py
@@ -106,7 +106,8 @@
     density = share * scale_factor
     centers = ((start + jnp.arange(share.shape[0], dtype=jnp.int32)).astype(jnp.float32) + 0.5) / NB
     for step in range(EM_ITERS):
-        sums = lax.psum(moments(share, centers, mean, var, weight), ("gy", "gx"))
+        array_in = moments(share, centers, mean, var, weight)
+        sums = lax.all_gather(array_in, ("gy", "gx")).sum(axis=0)
         mean, var, weight = refit(sums, float(phases))
     params = jnp.stack([mean, var, weight])
     intensity = (bins.astype(jnp.float32) + 0.5) / NB

time: 588 us -> 552 us (0.939)
  blocking collectives: 444 us -> 406 us
    psum x5 -> x0, blocking collectives: 369 us -> none  [per_device(): sums = lax.psum(moments(share, centers, mean, var, weight), ('gy', 'gx'))]
    all_gather x0 -> x5, blocking collectives: none -> 330 us  [per_device(): sums = lax.all_gather(array_in, ('gy', 'gx')).sum(axis=0)]
where the time goes in v1:
time: 552 us; the launch traced here: 551 us
  blocking collectives  406 us (74%)
  other arithmetic  64.7 us (12%)
  starting transfers between devices  34.1 us (6%)
  waiting for transfers between devices  32.4 us (6%)
  matrix products  6.88 us (1%)
    all_gather x5, blocking collectives, per_device(): sums = lax.all_gather(array_in, ('gy', 'gx')).sum(axis=0)  330 us
    unnamed x1, blocking collectives  75.7 us
    reduce_max x3, other arithmetic, per_device(): q = jax.nn.softmax(unary + BETA * field, axis=0).astype(jnp.bfloat16)  33.8 us
    ppermute x6, waiting for transfers between devices, extended(): after = lax.ppermute(initial, axis, down)  30.6 us
    ppermute x6, starting transfers between devices, extended(): before = lax.ppermute(last, axis, up)  19.4 us
    ppermute x6, starting transfers between devices, extended(): after = lax.ppermute(initial, axis, down)  14.6 us
  transfers between devices with their start and end apart: 12, of which 11 were waited for; matrix products, arithmetic and copies ran while one was open for 0% of the time, Pallas kernels for 0%

profile of v1, /device:TPU:121, one launch (start us, length us, event | category | flops | bytes accessed | tf_op | source)
XLA Modules:
  0.0 551.1 jit_solution(5134748434429618262)
XLA Ops:
  0.7 0.7 multiply_subtract_fusion
  1.3 0.7 fusion.37
  2.1 0.7 fusion.28
  2.8 1.0 add_multiply_fusion
  3.8 1.0 convert_element_type.292
  4.8 1.1 copy.9
  5.9 1.1 copy.8
  7.1 10.4 %while.13 = (s32[]{:T(128)}, f32[32,128]{1,0:T(8,128)S(1)}, s32[4,16384]{1,0:T(4,128)S(1)}, s32[4,16384]{1,0:T(4,128)S(1)}, s32[]{:T(128)}, /*index=5*/s32[]{:T(128)}) while((s32[]{:T(128)}, f32[32,128]{1,0:T(8,128)S(1)}, s32[4,16384]{1,0:T(4,128)S(1)}, s32[4,16384]{1,0:T(4,128)S(1)}, s32[]{:T(128)}, /*index=5*/s32[]{:T(128)}) %tuple.78), condition=%wide.region_3.4_spmd.clone, body=%wide.region_2.3_spmd.clone.sunk | while | flops 137715712 | bytes 2719839 | solution.py:97
  7.9 1.7 fusion.95
  10.5 1.7 fusion.95
  13.1 1.7 fusion.95
  15.7 1.7 fusion.95
  17.4 75.7 %all-reduce.3 = f32[4096]{0:T(1024)S(1)} all-reduce(f32[4096]{0:T(1024)S(1)} %bitcast.185), channel_id=7, replica_groups=mesh['gy'=32,'gx'=8] {'gy','gx'}, use_global_device_ids=true, to_apply=%region_4.5.clone | all-reduce | flops 4096 | bytes 32768
  94.0 66.7 %all-gather.5 = f32[256,3,8]{2,1,0:T(4,128)S(1)} all-gather(f32[1,3,8]{2,1,0:T(4,128)S(1)} %maximum_bitcast_fusion), channel_id=2, replica_groups=mesh['gy'=32,'gx'=8] {'gy','gx'}, dimensions={0}, use_global_device_ids=true | all-gather | bytes 24672 | tf_op jit(solution)/shard_map/all_gather | solution.py:110
  161.0 0.6 slice_reduce_fusion.4
  162.7 65.8 %all-gather.6 = f32[256,3,8]{2,1,0:T(4,128)S(1)} all-gather(f32[1,3,8]{2,1,0:T(4,128)S(1)} %maximum_bitcast_fusion.1), channel_id=3, replica_groups=mesh['gy'=32,'gx'=8] {'gy','gx'}, dimensions={0}, use_global_device_ids=true | all-gather | bytes 24672 | tf_op jit(solution)/shard_map/all_gather | solution.py:110
  230.6 65.7 %all-gather.7 = f32[256,3,8]{2,1,0:T(4,128)S(1)} all-gather(f32[1,3,8]{2,1,0:T(4,128)S(1)} %maximum_bitcast_fusion.2), channel_id=4, replica_groups=mesh['gy'=32,'gx'=8] {'gy','gx'}, dimensions={0}, use_global_device_ids=true | all-gather | bytes 24672 | tf_op jit(solution)/shard_map/all_gather | solution.py:110
  298.3 65.7 %all-gather.8 = f32[256,3,8]{2,1,0:T(4,128)S(1)} all-gather(f32[1,3,8]{2,1,0:T(4,128)S(1)} %maximum_bitcast_fusion.3), channel_id=5, replica_groups=mesh['gy'=32,'gx'=8] {'gy','gx'}, dimensions={0}, use_global_device_ids=true | all-gather | bytes 24672 | tf_op jit(solution)/shard_map/all_gather | solution.py:110
  366.0 65.9 %all-gather.9 = f32[256,3,8]{2,1,0:T(4,128)S(1)} all-gather(f32[1,3,8]{2,1,0:T(4,128)S(1)} %maximum_bitcast_fusion.4), channel_id=6, replica_groups=mesh['gy'=32,'gx'=8] {'gy','gx'}, dimensions={0}, use_global_device_ids=true | all-gather | bytes 24672 | tf_op jit(solution)/shard_map/all_gather | solution.py:110
  432.2 0.6 fusion.63
  434.0 0.7 fusion.18
  434.8 0.9 multiply_convert_fusion.3
  435.9 4.3 collective-permute-start
  440.2 1.9 collective-permute-start.1
  442.1 0.7 collective-permute-done
  442.9 7.2 %collective-permute-done.1 = bf16[8,4,2,1024]{3,2,1,0:T(2,128)(2,1)S(1)} collective-permute-done((bf16[8,4,2,1024]{3,2,1,0:T(2,128)(2,1)S(1)}, bf16[8,4,2,1024]{3,2,1,0:T(2,128)(2,1)S(1)}, u32[]{:S(2)}, u32[]{:S(2)}) %collective-permute-start.1) | collective-permute-done | bytes 131104 | tf_op jit(solution)/shard_map/ppermute | solution.py:22
  450.3 3.6 collective-permute-start.2
  453.9 1.9 collective-permute-start.3
  456.5 4.4 collective-permute-done.3
  460.9 2.9 maximum_maximum_fusion
  463.8 11.3 %fusion.75 = (f32[4,16,1024]{2,1,0:T(8,128)S(1)}, f32[8,4,16,1024]{3,2,1,0:T(8,128)S(1)}) fusion(f32[8,6,16,1024]{3,2,1,0:T(8,128)S(1)} %pad_convert_fusion.2, bf16[8,4,20,1026]{3,2,1,0:T(8,128)(2,1)S(1)} %get-tuple-element.134, bf16[8,4,2,1024]{3,2,1,0:T(2,128)(2,1)S(1)} %collective-permute-done.1, bf16[8,4,16,1024]{3,2,1,0:T(8,128)(2,1)S(1)} %multiply_convert_fusion.3, ...), kind=kLoop, calls=%fused_computation.201 | loop fusion | flops 47120384 | bytes 30146656 | tf_op jit(solution)/shard_map/reduce_max | solution.py:121
  476.1 1.9 collective-permute-start.4
  478.0 3.4 collective-permute-start.5
  481.8 5.2 collective-permute-done.5
  487.3 4.2 collective-permute-start.6
  491.4 2.1 collective-permute-start.7
  494.0 4.4 collective-permute-done.7
  498.4 2.9 maximum_maximum_fusion.1
  501.3 11.3 %fusion.73 = (f32[4,16,1024]{2,1,0:T(8,128)S(1)}, f32[8,4,16,1024]{3,2,1,0:T(8,128)S(1)}) fusion(f32[8,6,16,1024]{3,2,1,0:T(8,128)S(1)} %pad_convert_fusion.1, bf16[8,4,20,1026]{3,2,1,0:T(8,128)(2,1)S(1)} %get-tuple-element.130, bf16[8,4,2,1024]{3,2,1,0:T(2,128)(2,1)S(1)} %collective-permute-done.5, bf16[8,4,16,1024]{3,2,1,0:T(8,128)(2,1)S(1)} %multiply_convert_fusion.2, ...), kind=kLoop, calls=%fused_computation.200 | loop fusion | flops 47120384 | bytes 30146656 | tf_op jit(solution)/shard_map/reduce_max | solution.py:121
  513.6 1.9 collective-permute-start.8
  515.5 3.4 collective-permute-start.9
  519.5 5.1 collective-permute-done.9
  524.8 3.5 collective-permute-start.10
  528.3 1.9 collective-permute-start.11
  530.9 4.4 collective-permute-done.11
  535.3 2.9 maximum_maximum_fusion.2
  538.2 11.3 %fusion.71 = (f32[4,16,1024]{2,1,0:T(8,128)S(1)}, f32[8,4,16,1024]{3,2,1,0:T(8,128)S(1)}) fusion(f32[8,6,16,1024]{3,2,1,0:T(8,128)S(1)} %pad_convert_fusion, bf16[8,4,20,1026]{3,2,1,0:T(8,128)(2,1)S(1)} %get-tuple-element.126, bf16[8,4,2,1024]{3,2,1,0:T(2,128)(2,1)S(1)} %collective-permute-done.9, bf16[8,4,16,1024]{3,2,1,0:T(8,128)(2,1)S(1)} %multiply_convert_fusion.1, ...), kind=kLoop, calls=%fused_computation.199 | loop fusion | flops 47120384 | bytes 30146656 | tf_op jit(solution)/shard_map/reduce_max | solution.py:121
  549.7 1.4 multiply_convert_fusion
  (81 shorter events, 15.7 us)
Async XLA Ops:
  7.0 86.7 %copy-start.1 = (f32[8]{0:T(128)S(1)}, f32[8]{0:T(128)}, u32[]{:S(2)}) copy-start(f32[8]{0:T(128)} %param.10) | copy-start | bytes 100
  162.7 270.8 %copy-start = (bf16[8,4,16,1024]{3,2,1,0:T(8,128)(2,1)S(1)}, bf16[8,4,16,1024]{3,2,1,0:T(8,128)(2,1)}, u32[]{:S(2)}) copy-start(bf16[8,4,16,1024]{3,2,1,0:T(8,128)(2,1)} %param.9) | copy-start | bytes 3145732
  435.9 6.9 %collective-permute-start = (bf16[8,4,2,1024]{3,2,1,0:T(2,128)(2,1)S(1)}, bf16[8,4,2,1024]{3,2,1,0:T(2,128)(2,1)S(1)}, u32[]{:S(2)}, u32[]{:S(2)}) collective-permute-start(bf16[8,4,2,1024]{3,2,1,0:T(2,128)(2,1)S(1)} %get-tuple-element.141), channel_id=1, source_target_pairs={{0,8},{8,16},{16,24},{24,32},{32,40},{40,48},{48,56},{56,64},{64,7... | collective-permute-start | bytes 393224 | tf_op jit(solution)/shard_map/ppermute | solution.py:21
  440.2 9.8 %collective-permute-start.1 = (bf16[8,4,2,1024]{3,2,1,0:T(2,128)(2,1)S(1)}, bf16[8,4,2,1024]{3,2,1,0:T(2,128)(2,1)S(1)}, u32[]{:S(2)}, u32[]{:S(2)}) collective-permute-start(bf16[8,4,2,1024]{3,2,1,0:T(2,128)(2,1)S(1)} %get-tuple-element.142), channel_id=1, source_target_pairs={{8,0},{16,8},{24,16},{32,24},{40,32},{48,40},{56,48},{64,56},{72,6... | collective-permute-start | bytes 393224 | tf_op jit(solution)/shard_map/ppermute | solution.py:22
  450.3 6.2 %collective-permute-start.2 = (bf16[8,4,20,2]{3,2,1,0:T(8,128)(2,1)S(1)}, bf16[8,4,20,2]{3,2,1,0:T(8,128)(2,1)S(1)}, u32[]{:S(2)}, u32[]{:S(2)}) collective-permute-start(bf16[8,4,20,2]{3,2,1,0:T(8,128)(2,1)S(1)} %get-tuple-element.135), channel_id=1, source_target_pairs={{0,1},{1,2},{2,3},{3,4},{4,5},{5,6},{6,7},{8,9},{9,10},{10,11},{11... | collective-permute-start | bytes 7688 | tf_op jit(solution)/shard_map/ppermute | solution.py:21
  453.9 7.0 %collective-permute-start.3 = (bf16[8,4,20,2]{3,2,1,0:T(8,128)(2,1)S(1)}, bf16[8,4,20,2]{3,2,1,0:T(8,128)(2,1)S(1)}, u32[]{:S(2)}, u32[]{:S(2)}) collective-permute-start(bf16[8,4,20,2]{3,2,1,0:T(8,128)(2,1)S(1)} %get-tuple-element.136), channel_id=1, source_target_pairs={{1,0},{2,1},{3,2},{4,3},{5,4},{6,5},{7,6},{9,8},{10,9},{11,10},{12... | collective-permute-start | bytes 7688 | tf_op jit(solution)/shard_map/ppermute | solution.py:22
  476.1 5.7 %collective-permute-start.4 = (bf16[8,4,2,1024]{3,2,1,0:T(2,128)(2,1)S(1)}, bf16[8,4,2,1024]{3,2,1,0:T(2,128)(2,1)S(1)}, u32[]{:S(2)}, u32[]{:S(2)}) collective-permute-start(bf16[8,4,2,1024]{3,2,1,0:T(2,128)(2,1)S(1)} %get-tuple-element.139), channel_id=1, source_target_pairs={{0,8},{8,16},{16,24},{24,32},{32,40},{40,48},{48,56},{56,64},{64,7... | collective-permute-start | bytes 393224 | tf_op jit(solution)/shard_map/ppermute | solution.py:21
  478.0 9.0 %collective-permute-start.5 = (bf16[8,4,2,1024]{3,2,1,0:T(2,128)(2,1)S(1)}, bf16[8,4,2,1024]{3,2,1,0:T(2,128)(2,1)S(1)}, u32[]{:S(2)}, u32[]{:S(2)}) collective-permute-start(bf16[8,4,2,1024]{3,2,1,0:T(2,128)(2,1)S(1)} %get-tuple-element.140), channel_id=1, source_target_pairs={{8,0},{16,8},{24,16},{32,24},{40,32},{48,40},{56,48},{64,56},{72,6... | collective-permute-start | bytes 393224 | tf_op jit(solution)/shard_map/ppermute | solution.py:22
  487.3 6.8 %collective-permute-start.6 = (bf16[8,4,20,2]{3,2,1,0:T(8,128)(2,1)S(1)}, bf16[8,4,20,2]{3,2,1,0:T(8,128)(2,1)S(1)}, u32[]{:S(2)}, u32[]{:S(2)}) collective-permute-start(bf16[8,4,20,2]{3,2,1,0:T(8,128)(2,1)S(1)} %get-tuple-element.131), channel_id=1, source_target_pairs={{0,1},{1,2},{2,3},{3,4},{4,5},{5,6},{6,7},{8,9},{9,10},{10,11},{11... | collective-permute-start | bytes 7688 | tf_op jit(solution)/shard_map/ppermute | solution.py:21
  491.4 7.0 %collective-permute-start.7 = (bf16[8,4,20,2]{3,2,1,0:T(8,128)(2,1)S(1)}, bf16[8,4,20,2]{3,2,1,0:T(8,128)(2,1)S(1)}, u32[]{:S(2)}, u32[]{:S(2)}) collective-permute-start(bf16[8,4,20,2]{3,2,1,0:T(8,128)(2,1)S(1)} %get-tuple-element.132), channel_id=1, source_target_pairs={{1,0},{2,1},{3,2},{4,3},{5,4},{6,5},{7,6},{9,8},{10,9},{11,10},{12... | collective-permute-start | bytes 7688 | tf_op jit(solution)/shard_map/ppermute | solution.py:22
  513.6 5.9 %collective-permute-start.8 = (bf16[8,4,2,1024]{3,2,1,0:T(2,128)(2,1)S(1)}, bf16[8,4,2,1024]{3,2,1,0:T(2,128)(2,1)S(1)}, u32[]{:S(2)}, u32[]{:S(2)}) collective-permute-start(bf16[8,4,2,1024]{3,2,1,0:T(2,128)(2,1)S(1)} %get-tuple-element.137), channel_id=1, source_target_pairs={{0,8},{8,16},{16,24},{24,32},{32,40},{40,48},{48,56},{56,64},{64,7... | collective-permute-start | bytes 393224 | tf_op jit(solution)/shard_map/ppermute | solution.py:21
  515.5 9.0 %collective-permute-start.9 = (bf16[8,4,2,1024]{3,2,1,0:T(2,128)(2,1)S(1)}, bf16[8,4,2,1024]{3,2,1,0:T(2,128)(2,1)S(1)}, u32[]{:S(2)}, u32[]{:S(2)}) collective-permute-start(bf16[8,4,2,1024]{3,2,1,0:T(2,128)(2,1)S(1)} %get-tuple-element.138), channel_id=1, source_target_pairs={{8,0},{16,8},{24,16},{32,24},{40,32},{48,40},{56,48},{64,56},{72,6... | collective-permute-start | bytes 393224 | tf_op jit(solution)/shard_map/ppermute | solution.py:22
  524.8 6.1 %collective-permute-start.10 = (bf16[8,4,20,2]{3,2,1,0:T(8,128)(2,1)S(1)}, bf16[8,4,20,2]{3,2,1,0:T(8,128)(2,1)S(1)}, u32[]{:S(2)}, u32[]{:S(2)}) collective-permute-start(bf16[8,4,20,2]{3,2,1,0:T(8,128)(2,1)S(1)} %get-tuple-element.127), channel_id=1, source_target_pairs={{0,1},{1,2},{2,3},{3,4},{4,5},{5,6},{6,7},{8,9},{9,10},{10,11},{11... | collective-permute-start | bytes 7688 | tf_op jit(solution)/shard_map/ppermute | solution.py:21
  528.3 7.0 %collective-permute-start.11 = (bf16[8,4,20,2]{3,2,1,0:T(8,128)(2,1)S(1)}, bf16[8,4,20,2]{3,2,1,0:T(8,128)(2,1)S(1)}, u32[]{:S(2)}, u32[]{:S(2)}) collective-permute-start(bf16[8,4,20,2]{3,2,1,0:T(8,128)(2,1)S(1)} %get-tuple-element.128), channel_id=1, source_target_pairs={{1,0},{2,1},{3,2},{4,3},{5,4},{6,5},{7,6},{9,8},{10,9},{11,10},{12... | collective-permute-start | bytes 7688 | tf_op jit(solution)/shard_map/ppermute | solution.py:22
